TPU v7x, 32 devices: a whole 2x2x4 slice. The times are simulated.
32 devices in a mesh: dp: 8 (over z, x), tensor: 4 (over y, core).
Axes of the slice: x: 2, y: 2, z: 4, core: 2. Of those that a mesh axis runs over, the one named last changes fastest.
Arguments:
- layer_input: bfloat16 [16, 512, 2048], P('dp'), may hold values from -6 to 6
- segments: int32 [16, 512], P('dp'), may hold values from 0 to 3, never falling along the last dimension, each value on 1 to 256 neighbouring positions
- query_weight: bfloat16 [2048, 2048], P('dp', 'tensor'), may hold values from -0.125 to 0.125
- key_matrix: bfloat16 [2048, 1024], P('dp', 'tensor'), may hold values from -0.125 to 0.125
- value_matrix: bfloat16 [2048, 1024], P('dp', 'tensor'), may hold values from -0.125 to 0.125
- gate_weight: bfloat16 [2048, 2048], P('dp', 'tensor'), may hold values from -0.125 to 0.125
- out_weight: bfloat16 [2048, 2048], P('tensor', 'dp'), may hold values from -1 to 1
- ffn_gate_weight: bfloat16 [2048, 6144], P('dp', 'tensor'), may hold values from -0.125 to 0.125
- ffn_up_weight: bfloat16 [2048, 6144], P('dp', 'tensor'), may hold values from -0.125 to 0.125
- ffn_down_weight: bfloat16 [6144, 2048], P('tensor', 'dp'), may hold values from -0.109375 to 0.109375
- attn_gain: float32 [2048], replicated, may hold values from 0.5 to 1.5
- ffn_gain: float32 [2048], replicated, may hold values from 0.5 to 1.5
- query_gain: float32 [128], replicated, may hold values from 0.1 to 1.9
- key_norm_gain: float32 [128], replicated, may hold values from 0.1 to 1.9
- cotangent: bfloat16 [16, 512, 2048], P('dp'), may hold values from -6 to 6
Outputs:
- output: bfloat16 [16, 512, 2048], P('dp')
- input_grad: float32 [16, 512, 2048], P('dp')
- grad_query_weight: float32 [2048, 2048], P('dp', 'tensor')
- grad_key_weight: float32 [2048, 1024], P('dp', 'tensor')
- grad_value_weight: float32 [2048, 1024], P('dp', 'tensor')
- grad_gate_weight: float32 [2048, 2048], P('dp', 'tensor')
- grad_out_weight: float32 [2048, 2048], P('tensor', 'dp')
- grad_ffn_gate_weight: float32 [2048, 6144], P('dp', 'tensor')
- grad_ffn_up_weight: float32 [2048, 6144], P('dp', 'tensor')
- grad_ffn_down_weight: float32 [6144, 2048], P('tensor', 'dp')
- grad_attn_gain: float32 [2048], replicated
- grad_ffn_gain: float32 [2048], replicated
- grad_query_gain: float32 [128], replicated
- grad_key_gain: float32 [128], replicated
Inputs may be any that keep to these rules, and one draw needn't show every extreme that they name: `segments`: segment numbers never fall along a sequence; each document holds 1 to 256 tokens and some document holds exactly 256.
All inputs are finite; a program needn't handle non-finite values.
Results may differ from a plain program's by a relative error of at most 0.02.
Values may be sent and summed in bfloat16 or wider, within the bound.
No kernel may reach another device: no remote copies, remote signals or barrier semaphores. Data moves between devices by JAX's collectives and lax.ppermute only.
A program may use at most 256 MiB of HBM per device.

v0:
```python
import math
import jax
import jax.numpy as jnp
from jax import lax
from jax.sharding import PartitionSpec as P

epsilon = 1e-06


def norm_fwd(vector_in):
    scale_inv = lax.rsqrt(jnp.mean(vector_in * vector_in, axis=-1, keepdims=True) + epsilon)
    return (vector_in * scale_inv, scale_inv)


def norm_back(normal, scale_inv, gain_vec, grad_in_rows, tensor_rank, share_rows):
    scaled = grad_in_rows * gain_vec
    grad_rows = scale_inv * (scaled - normal * jnp.mean(scaled * normal, axis=-1, keepdims=True))
    grad_gain = jnp.sum(
        lax.dynamic_slice_in_dim(grad_in_rows * normal, tensor_rank * share_rows, share_rows, 0),
        axis=0,
    )
    return (grad_rows, grad_gain)


def rotary_apply(vector_in, cosine_table, sine_table):
    halfway = vector_in.shape[-1] // 2
    turned = jnp.concatenate([-vector_in[..., halfway:], vector_in[..., :halfway]], axis=-1)
    return vector_in * cosine_table + turned * sine_table


def tables(segment_row, head_size):
    token_length = segment_row.shape[0]
    places = jnp.arange(token_length, dtype=jnp.int32)
    changed = jnp.concatenate(
        [jnp.ones((1,), dtype=jnp.bool_), segment_row[1:] != segment_row[:-1]]
    )
    starts = lax.cummax(jnp.where(changed, places, jnp.zeros_like(places)), axis=0)
    position = (places - starts).astype(jnp.float32)
    frequency = jnp.exp(
        jnp.arange(head_size // 2, dtype=jnp.float32) * (-2.0 * math.log(1000000.0) / head_size)
    )
    angles = position[:, None] * frequency[None, :]
    angles = jnp.concatenate([angles, angles], axis=-1)
    allowed = (segment_row[:, None] == segment_row[None, :]) & (places[None, :] <= places[:, None])
    return (jnp.cos(angles)[:, None, :], jnp.sin(angles)[:, None, :], allowed)


def layer_pass(
    seq_input,
    seg_row,
    grad_out,
    gathered,
    attn_gain,
    ffn_gain,
    query_gain,
    key_norm_gain,
    tensor_rank,
    share_rows,
):
    full_q, full_k, full_v, full_g, full_o, full_gf, full_up, full_dn = gathered
    head_size = query_gain.shape[0]
    token_length = seq_input.shape[0]
    heads_q = full_q.shape[1] // head_size
    heads_kv = full_k.shape[1] // head_size
    group_width = heads_q // heads_kv
    scaling = head_size ** (-0.5)
    low_type = jnp.bfloat16
    wide_type = jnp.float32
    cosine_table, sine_table, allowed = tables(seg_row, head_size)
    normal_one, inv_one = norm_fwd(seq_input)
    first_normed = (normal_one * attn_gain).astype(low_type)
    query_proj = jnp.dot(first_normed, full_q, preferred_element_type=wide_type)
    key_projected = jnp.dot(first_normed, full_k, preferred_element_type=wide_type)
    value_projected = jnp.dot(first_normed, full_v, preferred_element_type=wide_type)
    gate_proj = jnp.dot(first_normed, full_g, preferred_element_type=wide_type)

    def prepare(query_in, key_in, gain_q, gain_k):
        query_n = norm_fwd(query_in.reshape(token_length, heads_q, head_size))[0] * gain_q
        key_n = norm_fwd(key_in.reshape(token_length, heads_kv, head_size))[0] * gain_k
        return (
            rotary_apply(query_n, cosine_table, sine_table),
            rotary_apply(key_n, cosine_table, sine_table),
        )

    (query_full, key_full), prepare_back = jax.vjp(
        prepare, query_proj, key_projected, query_gain, key_norm_gain
    )
    query_low = query_full.astype(low_type).reshape(token_length, heads_kv, group_width, head_size)
    key_low = key_full.astype(low_type)
    value_low = value_projected.astype(low_type).reshape(token_length, heads_kv, head_size)
    raw_scores = jnp.einsum("skgd,tkd->kgst", query_low, key_low, preferred_element_type=wide_type)
    scores = jnp.where(allowed, raw_scores * scaling, -1000000000.0)
    highest = jnp.max(scores, axis=-1, keepdims=True)
    exponent = jnp.exp(scores - highest)
    row_total = jnp.sum(exponent, axis=-1, keepdims=True)
    softmaxed = exponent / row_total
    log_total = highest + jnp.log(row_total)
    attended = jnp.einsum(
        "kgst,tkd->skgd", softmaxed.astype(low_type), value_low, preferred_element_type=wide_type
    ).reshape(token_length, heads_q * head_size)
    gate_sig = jax.nn.sigmoid(gate_proj)
    gated = (attended * gate_sig).astype(low_type)
    branch_one = lax.psum(jnp.dot(gated, full_o, preferred_element_type=wide_type), "tensor")
    middle = seq_input + branch_one
    normal_two, inv_two = norm_fwd(middle)
    second_normed = (normal_two * ffn_gain).astype(low_type)
    ffn_gate = jnp.dot(second_normed, full_gf, preferred_element_type=wide_type)
    ffn_up = jnp.dot(second_normed, full_up, preferred_element_type=wide_type)
    sig_gate = jax.nn.sigmoid(ffn_gate)
    active = ffn_gate * sig_gate
    hidden = (active * ffn_up).astype(low_type)
    branch_two = lax.psum(
        jnp.dot(hidden, full_dn, preferred_element_type=wide_type).astype(jnp.bfloat16), "tensor"
    ).astype(jnp.float32)
    result = (middle + branch_two).astype(low_type)
    grad_low = grad_out.astype(low_type)
    grad_dn = jnp.einsum("sf,sd->fd", hidden, grad_low, preferred_element_type=wide_type)
    grad_hidden = jnp.einsum("sd,fd->sf", grad_low, full_dn, preferred_element_type=wide_type)
    grad_ffn_gate = (grad_hidden * ffn_up * sig_gate * (1.0 + ffn_gate * (1.0 - sig_gate))).astype(
        low_type
    )
    grad_ffn_up = (grad_hidden * active).astype(low_type)
    grad_gf = jnp.einsum(
        "sd,sf->df", second_normed, grad_ffn_gate, preferred_element_type=wide_type
    )
    grad_up = jnp.einsum("sd,sf->df", second_normed, grad_ffn_up, preferred_element_type=wide_type)
    part_two = jnp.einsum(
        "sf,df->sd", grad_ffn_gate, full_gf, preferred_element_type=wide_type
    ) + jnp.einsum("sf,df->sd", grad_ffn_up, full_up, preferred_element_type=wide_type)
    grad_second = lax.psum(part_two, "tensor")
    back_two, grad_ffn_gain = norm_back(
        normal_two, inv_two, ffn_gain, grad_second, tensor_rank, share_rows
    )
    grad_middle = grad_out + back_two
    middle_low = grad_middle.astype(low_type)
    grad_o = jnp.einsum("sf,sd->fd", gated, middle_low, preferred_element_type=wide_type)
    grad_gated = (
        jnp.einsum("sd,fd->sf", middle_low, full_o, preferred_element_type=wide_type)
        .astype(low_type)
        .astype(wide_type)
    )
    grad_attended = (
        (grad_gated * gate_sig)
        .astype(low_type)
        .reshape(token_length, heads_kv, group_width, head_size)
    )
    grad_gate_proj = (grad_gated * attended * gate_sig * (1.0 - gate_sig)).astype(low_type)
    raw_again = jnp.einsum("skgd,tkd->kgst", query_low, key_low, preferred_element_type=wide_type)
    probs_again = jnp.exp(jnp.where(allowed, raw_again * scaling, -1000000000.0) - log_total)
    grad_value = (
        jnp.einsum(
            "kgst,skgd->tkd",
            probs_again.astype(low_type),
            grad_attended,
            preferred_element_type=wide_type,
        )
        .astype(low_type)
        .reshape(token_length, heads_kv * head_size)
    )
    grad_probs = jnp.einsum(
        "skgd,tkd->kgst", grad_attended, value_low, preferred_element_type=wide_type
    )
    grad_scores = (
        probs_again
        * (grad_probs - jnp.sum(probs_again * grad_probs, axis=-1, keepdims=True))
        * scaling
    ).astype(low_type)
    grad_queries = jnp.einsum(
        "kgst,tkd->skgd", grad_scores, key_low, preferred_element_type=wide_type
    ).reshape(token_length, heads_q, head_size)
    grad_keys = jnp.einsum(
        "kgst,skgd->tkd", grad_scores, query_low, preferred_element_type=wide_type
    )
    grad_query_proj, grad_key_proj, grad_query_gain, grad_key_gain = prepare_back(
        (grad_queries, grad_keys)
    )
    grad_query_low = grad_query_proj.astype(low_type)
    grad_key_low = grad_key_proj.astype(low_type)
    grad_q = jnp.einsum("sd,sf->df", first_normed, grad_query_low, preferred_element_type=wide_type)
    grad_k = jnp.einsum("sd,sf->df", first_normed, grad_key_low, preferred_element_type=wide_type)
    grad_v = jnp.einsum("sd,sf->df", first_normed, grad_value, preferred_element_type=wide_type)
    grad_g = jnp.einsum("sd,sf->df", first_normed, grad_gate_proj, preferred_element_type=wide_type)
    part_one = (
        jnp.einsum("sf,df->sd", grad_query_low, full_q, preferred_element_type=wide_type)
        + jnp.einsum("sf,df->sd", grad_key_low, full_k, preferred_element_type=wide_type)
        + jnp.einsum("sf,df->sd", grad_value, full_v, preferred_element_type=wide_type)
        + jnp.einsum("sf,df->sd", grad_gate_proj, full_g, preferred_element_type=wide_type)
    )
    grad_first = lax.psum(part_one.astype(jnp.bfloat16), "tensor").astype(jnp.float32)
    back_one, grad_attn_gain = norm_back(
        normal_one, inv_one, attn_gain, grad_first, tensor_rank, share_rows
    )
    grad_input = grad_middle + back_one
    return (
        result,
        grad_input,
        (grad_q, grad_k, grad_v, grad_g, grad_o, grad_gf, grad_up, grad_dn),
        (grad_attn_gain, grad_ffn_gain, grad_query_gain, grad_key_gain),
    )


def shards(
    layer_input,
    segments,
    query_weight,
    key_matrix,
    value_matrix,
    gate_weight,
    out_weight,
    ffn_gate_weight,
    ffn_up_weight,
    ffn_down_weight,
    attn_gain,
    ffn_gain,
    query_gain,
    key_norm_gain,
    cotangent,
):
    tensor_rank = lax.axis_index("tensor")
    share_rows = layer_input.shape[1] // lax.axis_size("tensor")
    gathered = (
        query_weight,
        key_matrix,
        value_matrix,
        gate_weight,
        out_weight,
        ffn_gate_weight,
        ffn_up_weight,
        ffn_down_weight,
    )
    totals = None
    gain_totals = (
        jnp.zeros_like(attn_gain),
        jnp.zeros_like(ffn_gain),
        jnp.zeros_like(query_gain),
        jnp.zeros_like(key_norm_gain),
    )
    results = []
    input_grads = []
    for micro_step in range(layer_input.shape[0]):
        gathered = (
            lax.all_gather(query_weight, "dp", axis=0, tiled=True),
            lax.all_gather(key_matrix, "dp", axis=0, tiled=True),
            lax.all_gather(value_matrix, "dp", axis=0, tiled=True),
            lax.all_gather(gate_weight, "dp", axis=0, tiled=True),
            lax.all_gather(out_weight, "dp", axis=1, tiled=True),
            lax.all_gather(ffn_gate_weight, "dp", axis=0, tiled=True),
            lax.all_gather(ffn_up_weight, "dp", axis=0, tiled=True),
            lax.all_gather(ffn_down_weight, "dp", axis=1, tiled=True),
        )
        result, grad_input, grads, gain_grads = layer_pass(
            layer_input[micro_step].astype(jnp.float32),
            segments[micro_step],
            cotangent[micro_step].astype(jnp.float32),
            gathered,
            attn_gain,
            ffn_gain,
            query_gain,
            key_norm_gain,
            tensor_rank,
            share_rows,
        )
        if totals is None:
            totals = grads
        else:
            totals = tuple((running + adding for running, adding in zip(totals, grads)))
        gain_totals = tuple((running + adding for running, adding in zip(gain_totals, gain_grads)))
        results.append(result)
        input_grads.append(grad_input)
    totals = (
        lax.psum_scatter(
            totals[0].astype(jnp.bfloat16), "dp", scatter_dimension=0, tiled=True
        ).astype(jnp.float32),
        lax.psum_scatter(
            totals[1].astype(jnp.bfloat16), "dp", scatter_dimension=0, tiled=True
        ).astype(jnp.float32),
        lax.psum_scatter(
            totals[2].astype(jnp.bfloat16), "dp", scatter_dimension=0, tiled=True
        ).astype(jnp.float32),
        lax.psum_scatter(
            totals[3].astype(jnp.bfloat16), "dp", scatter_dimension=0, tiled=True
        ).astype(jnp.float32),
        lax.psum_scatter(
            totals[4].astype(jnp.bfloat16), "dp", scatter_dimension=1, tiled=True
        ).astype(jnp.float32),
        lax.psum_scatter(
            totals[5].astype(jnp.bfloat16), "dp", scatter_dimension=0, tiled=True
        ).astype(jnp.float32),
        lax.psum_scatter(
            totals[6].astype(jnp.bfloat16), "dp", scatter_dimension=0, tiled=True
        ).astype(jnp.float32),
        lax.psum_scatter(
            totals[7].astype(jnp.bfloat16), "dp", scatter_dimension=1, tiled=True
        ).astype(jnp.float32),
    )
    sum_attn_gain, sum_ffn_gain, sum_query_gain, sum_key_gain = lax.psum(
        gain_totals, ("dp", "tensor")
    )
    return (
        jnp.stack(results),
        jnp.stack(input_grads),
        totals[0],
        totals[1],
        totals[2],
        totals[3],
        totals[4],
        totals[5],
        totals[6],
        totals[7],
        sum_attn_gain,
        sum_ffn_gain,
        sum_query_gain,
        sum_key_gain,
    )


def solution(mesh):
    return jax.shard_map(
        shards,
        mesh=mesh,
        in_specs=(
            P("dp", None, None),
            P("dp", None),
            P("dp", "tensor"),
            P("dp", "tensor"),
            P("dp", "tensor"),
            P("dp", "tensor"),
            P("tensor", "dp"),
            P("dp", "tensor"),
            P("dp", "tensor"),
            P("tensor", "dp"),
            P(),
            P(),
            P(),
            P(),
            P("dp", None, None),
        ),
        out_specs=(
            P("dp", None, None),
            P("dp", None, None),
            P("dp", "tensor"),
            P("dp", "tensor"),
            P("dp", "tensor"),
            P("dp", "tensor"),
            P("tensor", "dp"),
            P("dp", "tensor"),
            P("dp", "tensor"),
            P("tensor", "dp"),
            P(),
            P(),
            P(),
            P(),
        ),
        check_vma=False,
    )
```

profile of v0, /device:TPU:0, one launch (start us, length us, event | category | flops | bytes accessed | tf_op | source)
XLA Modules:
  0.0 1850.4 jit_solution(13215816996098095445)
XLA Ops:
  13.6 3.1 fusion.8
  19.3 33.9 %all-gather.11.cloned.1.call-done = bf16[2048,256]{1,0:T(8,128)(2,1)} async-done(((bf16[256,256]{1,0:T(8,128)(2,1)}), bf16[2048,256]{1,0:T(8,128)(2,1)}) %all-gather.11.cloned.1.call-update) | async-done | bytes 1048592 | tf_op jit(solution)/shard_map/all_gather | solution.py:243
  59.6 34.7 %all-gather.9.cloned.1.call-done = bf16[2048,256]{1,0:T(8,128)(2,1)} async-done(((bf16[256,256]{1,0:T(8,128)(2,1)}), bf16[2048,256]{1,0:T(8,128)(2,1)}) %all-gather.9.cloned.1.call-update) | async-done | bytes 1048592 | tf_op jit(solution)/shard_map/all_gather | solution.py:244
  94.3 2.9 convolution_convert_fusion.4
  98.7 45.6 %all-gather.13.cloned.1.call-done = bf16[2048,512]{1,0:T(8,128)(2,1)} async-done(((bf16[256,512]{1,0:T(8,128)(2,1)}), bf16[2048,512]{1,0:T(8,128)(2,1)}) %all-gather.13.cloned.1.call-update) | async-done | bytes 2097168 | tf_op jit(solution)/shard_map/all_gather | solution.py:242
  144.3 4.3 copy.48
  148.7 3.7 multiply_reduce_fusion.10
  162.4 31.5 %all-gather.15.cloned.1.call-done = bf16[2048,512]{1,0:T(8,128)(2,1)} async-done(((bf16[256,512]{1,0:T(8,128)(2,1)}), bf16[2048,512]{1,0:T(8,128)(2,1)}) %all-gather.15.cloned.1.call-update) | async-done | bytes 2097168 | tf_op jit(solution)/shard_map/all_gather | solution.py:245
  193.9 4.9 fusion.115
  204.9 39.8 %all-gather.17.cloned.1.call-done = bf16[512,2048]{1,0:T(8,128)(2,1)} async-done(((bf16[512,256]{1,0:T(8,128)(2,1)}), bf16[512,2048]{1,0:T(8,128)(2,1)}) %all-gather.17.cloned.1.call-update) | async-done | bytes 2097168 | tf_op jit(solution)/shard_map/all_gather | solution.py:246
  244.7 5.2 fusion.178
  249.9 3.3 fusion.175
  255.5 148.9 %all-reduce.18.cloned.1.call-done = (f32[512,2048]{1,0:T(8,128)}, f32[512,2048]{1,0:T(8,128)}) async-done(((f32[512,2048]{1,0:T(8,128)}, f32[512,2048]{1,0:T(8,128)}), (f32[512,2048]{1,0:T(8,128)}, f32[512,2048]{1,0:T(8,128)})) %all-reduce.18.cloned.1.call-update) | async-done | bytes 8388624 | tf_op jit(solution)/shard_map/psum | solution.py:103
  404.5 5.9 multiply_reduce_fusion.5
  412.7 5.4 multiply_convert_fusion.2
  418.1 87.4 %all-gather.21.cloned.1.call-done = bf16[2048,1536]{1,0:T(8,128)(2,1)} async-done(((bf16[256,1536]{1,0:T(8,128)(2,1)}), bf16[2048,1536]{1,0:T(8,128)(2,1)}) %all-gather.21.cloned.1.call-update) | async-done | bytes 6291472 | tf_op jit(solution)/shard_map/all_gather | solution.py:248
  505.5 8.5 fusion.177
  514.0 90.6 %all-gather.19.cloned.1.call-done = bf16[2048,1536]{1,0:T(8,128)(2,1)} async-done(((bf16[256,1536]{1,0:T(8,128)(2,1)}), bf16[2048,1536]{1,0:T(8,128)(2,1)}) %all-gather.19.cloned.1.call-update) | async-done | bytes 6291472 | tf_op jit(solution)/shard_map/all_gather | solution.py:247
  604.6 8.6 fusion.176
  613.2 5.1 fusion.180
  618.3 5.1 fusion.179
  623.4 81.0 %all-gather.23.cloned.1.call-done = bf16[1536,2048]{1,0:T(8,128)(2,1)} async-done(((bf16[1536,256]{1,0:T(8,128)(2,1)}), bf16[1536,2048]{1,0:T(8,128)(2,1)}) %all-gather.23.cloned.1.call-update) | async-done | bytes 6291472 | tf_op jit(solution)/shard_map/all_gather | solution.py:249
  704.3 11.4 multiply_convert_fusion.4
  716.8 8.3 fusion.186
  725.1 7.7 multiply_convert_fusion.6
  732.9 6.7 fusion.181
  739.6 7.9 convolution_add_fusion.1
  747.6 5.1 convolution_add_fusion
  752.8 8.1 convolution_convert_fusion.1
  760.9 7.4 convolution_convert_fusion
  768.4 135.6 %all-reduce.16.cloned.1.call-done = (f32[512,2048]{1,0:T(8,128)}, f32[512,2048]{1,0:T(8,128)}) async-done(((f32[512,2048]{1,0:T(8,128)}, f32[512,2048]{1,0:T(8,128)}), (f32[512,2048]{1,0:T(8,128)}, f32[512,2048]{1,0:T(8,128)})) %all-reduce.16.cloned.1.call-update) | async-done | bytes 8388624 | tf_op jit(solution)/shard_map/psum | solution.py:130
  903.9 6.9 multiply_reduce_fusion.3
  913.4 6.0 multiply_add_fusion
  921.7 2.9 fusion.187
  926.6 9.0 broadcast_multiply_fusion.2
  935.7 9.0 fusion.61
  944.7 4.7 fusion.97
  949.4 2.9 fusion.182
  953.7 9.1 broadcast_multiply_fusion.3
  962.8 9.3 fusion.67
  1004.2 3.7 fusion.120
  1010.8 3.2 fusion.52
  1014.0 2.8 add_convert_fusion.5
  1016.9 3.2 fusion.155
  1020.2 2.9 add_convert_fusion.4
  1023.2 5.8 fusion.192
  1028.9 5.6 add_convert_fusion.1
  1034.7 5.7 fusion.191
  1040.4 5.7 add_convert_fusion.2
  1047.5 5.2 fusion.37
  1052.8 7.2 add_convert_fusion
  1065.0 43.2 %reduce-scatter.11.cloned.1.call-done = bf16[256,256]{1,0:T(8,128)(2,1)} async-done(((bf16[2048,256]{1,0:T(8,128)(2,1)}), bf16[256,256]{1,0:T(8,128)(2,1)}) %reduce-scatter.11.cloned.1.call-update) | async-done | bytes 131088 | tf_op jit(solution)/shard_map/reduce_scatter | solution.py:274
  1109.8 153.5 %all-reduce.20.cloned.1.call-done = (bf16[512,2048]{1,0:T(8,128)(2,1)}, bf16[512,2048]{1,0:T(8,128)(2,1)}, bf16[512,2048]{1,0:T(8,128)(2,1)}, bf16[512,2048]{1,0:T(8,128)(2,1)}) async-done(((bf16[512,2048]{1,0:T(8,128)(2,1)}, bf16[512,2048]{1,0:T(8,128)(2,1)}, bf16[512,2048]{1,0:T(8,128)(2,1)}, bf16[512,2048]{1,0:T(8,128)(2,1)}), (bf16[512,2048]{1,0:T(8,128)(2,1)}, bf16[512,2048]{1,0:T(8,128)(2,1)}, ...) | async-done | bytes 8388624 | tf_op jit(solution)/shard_map/psum | solution.py:112
  1263.3 4.2 convert_element_type.355
  1273.9 17.2 add_bitcast_fusion.1
  1294.6 41.1 %reduce-scatter.17.cloned.1.call-done = bf16[512,256]{1,0:T(8,128)(2,1)} async-done(((bf16[512,2048]{1,0:T(8,128)(2,1)}), bf16[512,256]{1,0:T(8,128)(2,1)}) %reduce-scatter.17.cloned.1.call-update) | async-done | bytes 262160 | tf_op jit(solution)/shard_map/reduce_scatter | solution.py:283
  1337.5 69.2 %reduce-scatter.9.cloned.1.call-done = bf16[256,512]{1,0:T(8,128)(2,1)} async-done(((bf16[2048,512]{1,0:T(8,128)(2,1)}), bf16[256,512]{1,0:T(8,128)(2,1)}) %reduce-scatter.9.cloned.1.call-update) | async-done | bytes 262160 | tf_op jit(solution)/shard_map/reduce_scatter | solution.py:271
  1408.5 69.0 %reduce-scatter.15.cloned.1.call-done = bf16[256,512]{1,0:T(8,128)(2,1)} async-done(((bf16[2048,512]{1,0:T(8,128)(2,1)}), bf16[256,512]{1,0:T(8,128)(2,1)}) %reduce-scatter.15.cloned.1.call-update) | async-done | bytes 262160 | tf_op jit(solution)/shard_map/reduce_scatter | solution.py:280
  1479.3 43.3 %all-reduce.8 = (f32[2048]{0:T(1024)}, f32[2048]{0:T(1024)}, f32[128]{0:T(128)}, f32[128]{0:T(128)}) all-reduce(f32[2048]{0:T(1024)S(1)} %add.311, f32[2048]{0:T(1024)S(1)} %add.312, f32[128]{0:T(128)S(1)} %add.313, f32[128]{0:T(128)S(1)} %add.314), channel_id=1, replica_groups=mesh['dp'=8,'tensor'=4] {'dp','tensor'}, use_global_device_ids=true, to_apply=%region_44.45 | all-reduce | flops 4352 | bytes 34816 | tf_op jit(solution)/shard_map/psum | solution.py:296
  1522.6 4.3 pad_maximum_fusion.1
  1528.3 4.0 pad_maximum_fusion
  1532.2 66.7 %reduce-scatter.21.cloned.1.call-done = bf16[256,1536]{1,0:T(8,128)(2,1)} async-done(((bf16[2048,1536]{1,0:T(8,128)(2,1)}), bf16[256,1536]{1,0:T(8,128)(2,1)}) %reduce-scatter.21.cloned.1.call-update) | async-done | bytes 786448 | tf_op jit(solution)/shard_map/reduce_scatter | solution.py:289
  1601.4 118.3 %reduce-scatter.19.cloned.1.call-done = bf16[256,1536]{1,0:T(8,128)(2,1)} async-done(((bf16[2048,1536]{1,0:T(8,128)(2,1)}), bf16[256,1536]{1,0:T(8,128)(2,1)}) %reduce-scatter.19.cloned.1.call-update) | async-done | bytes 786448 | tf_op jit(solution)/shard_map/reduce_scatter | solution.py:286
  1722.2 118.9 %reduce-scatter.23.cloned.1.call-done = bf16[1536,256]{1,0:T(8,128)(2,1)} async-done(((bf16[1536,2048]{1,0:T(8,128)(2,1)}), bf16[1536,256]{1,0:T(8,128)(2,1)}) %reduce-scatter.23.cloned.1.call-update) | async-done | bytes 786448 | tf_op jit(solution)/shard_map/reduce_scatter | solution.py:292
  (419 shorter events, 113.1 us)
Async XLA Ops:
  7.2 46.0 %all-gather.11.cloned.1.call-start = ((), (), s32[]{:S(2)}) async-start(), calls=%async_computation.9 | async-start | bytes 1179648 | tf_op jit(solution)/shard_map/all_gather | solution.py:243
  7.9 86.4 %all-gather.9.cloned.1.call-start = ((), (), s32[]{:S(2)}) async-start(), calls=%async_computation.8 | async-start | bytes 1179648 | tf_op jit(solution)/shard_map/all_gather | solution.py:244
  8.7 135.6 %all-gather.13.cloned.1.call-start = ((), (), s32[]{:S(2)}) async-start(), calls=%async_computation.10 | async-start | bytes 2359296 | tf_op jit(solution)/shard_map/all_gather | solution.py:242
  9.4 184.5 %all-gather.15.cloned.1.call-start = ((), (), s32[]{:S(2)}) async-start(), calls=%async_computation.11 | async-start | bytes 2359296 | tf_op jit(solution)/shard_map/all_gather | solution.py:245
  10.0 234.7 %all-gather.17.cloned.1.call-start = ((), (), s32[]{:S(2)}) async-start(), calls=%async_computation.12 | async-start | bytes 2359296 | tf_op jit(solution)/shard_map/all_gather | solution.py:246
  10.6 393.9 %all-reduce.18.cloned.1.call-start = ((), (), s32[]{:S(2)}) async-start(), calls=%async_computation.25 | async-start | bytes 16777216 | tf_op jit(solution)/shard_map/psum | solution.py:103
  13.6 41.0 %copy-start.109 = (f32[2048]{0:T(1024)S(1)}, f32[2048]{0:T(1024)}, u32[]{:S(2)}) copy-start(f32[2048]{0:T(1024)} %param.25) | copy-start | bytes 24580
  18.2 138.5 %copy-start.36 = (f32[512,128]{0,1:T(8,128)}, f32[512,128]{0,1:T(8,128)S(1)}, u32[]{:S(2)}) copy-start(f32[512,128]{0,1:T(8,128)S(1)} %get-tuple-element.88) | copy-start | bytes 786436
  18.2 138.5 %copy-start.48 = (f32[512,128]{0,1:T(8,128)}, f32[512,128]{0,1:T(8,128)S(1)}, u32[]{:S(2)}) copy-start(f32[512,128]{0,1:T(8,128)S(1)} %get-tuple-element.89) | copy-start | bytes 786436
  19.2 136.1 %copy-start.38 = (f32[512,128]{0,1:T(8,128)}, f32[512,128]{0,1:T(8,128)S(1)}, u32[]{:S(2)}) copy-start(f32[512,128]{0,1:T(8,128)S(1)} %get-tuple-element.90) | copy-start | bytes 786436
  19.2 136.1 %copy-start.46 = (f32[512,128]{0,1:T(8,128)}, f32[512,128]{0,1:T(8,128)S(1)}, u32[]{:S(2)}) copy-start(f32[512,128]{0,1:T(8,128)S(1)} %get-tuple-element.91) | copy-start | bytes 786436
  19.3 174.6 %copy-start.113 = (f32[512]{0:T(512)}, f32[512]{0:T(512)S(1)}, u32[]{:S(2)}) copy-start(f32[512]{0:T(512)S(1)} %get-tuple-element.131) | copy-start | bytes 6148
  19.3 180.5 %copy-start.111 = (f32[512]{0:T(512)}, f32[512]{0:T(512)S(1)}, u32[]{:S(2)}) copy-start(f32[512]{0:T(512)S(1)} %get-tuple-element.130) | copy-start | bytes 6148
  59.4 98.3 %copy-start.86 = (bf16[512,2,128,1]{0,2,3,1:T(8,128)(2,1)}, bf16[512,2,128,1]{0,2,3,1:T(8,128)(2,1)S(1)}, u32[]{:S(2)}) copy-start(bf16[512,2,128,1]{0,2,3,1:T(8,128)(2,1)S(1)} %fusion.131) | copy-start | bytes 786436
  59.6 96.1 %copy-start.84 = (bf16[512,2,128,1]{0,2,3,1:T(8,128)(2,1)}, bf16[512,2,128,1]{0,2,3,1:T(8,128)(2,1)S(1)}, u32[]{:S(2)}) copy-start(bf16[512,2,128,1]{0,2,3,1:T(8,128)(2,1)S(1)} %fusion.132) | copy-start | bytes 786436
  97.7 101.1 %copy-start.94 = (bf16[512,256]{0,1:T(8,128)(2,1)}, bf16[512,256]{0,1:T(8,128)(2,1)S(1)}, u32[]{:S(2)}) copy-start(bf16[512,256]{0,1:T(8,128)(2,1)S(1)} %convolution_convert_fusion.4) | copy-start | bytes 786436
  98.7 62.8 %copy-start.92 = (bf16[512,256]{0,1:T(8,128)(2,1)}, bf16[512,256]{0,1:T(8,128)(2,1)S(1)}, u32[]{:S(2)}) copy-start(bf16[512,256]{0,1:T(8,128)(2,1)S(1)} %convolution_convert_fusion.5) | copy-start | bytes 786436
  162.4 36.4 %copy-start.64 = (f32[2,128,2,512]{3,1,2,0:T(8,128)}, f32[2,128,2,512]{3,1,2,0:T(8,128)S(1)}, u32[]{:S(2)}) copy-start(f32[2,128,2,512]{3,1,2,0:T(8,128)S(1)} %fusion.68) | copy-start | bytes 3145732
  198.8 51.1 %copy-start.62 = (bf16[512,512]{0,1:T(8,128)(2,1)}, bf16[512,512]{0,1:T(8,128)(2,1)S(1)}, u32[]{:S(2)}) copy-start(bf16[512,512]{0,1:T(8,128)(2,1)S(1)} %get-tuple-element.120) | copy-start | bytes 1572868
  204.9 48.3 %copy-start.76 = (bf16[512,512]{0,1:T(8,128)(2,1)}, bf16[512,512]{0,1:T(8,128)(2,1)S(1)}, u32[]{:S(2)}) copy-start(bf16[512,512]{0,1:T(8,128)(2,1)S(1)} %get-tuple-element.124) | copy-start | bytes 1572868
  253.2 252.3 %all-gather.21.cloned.1.call-start = ((), (), s32[]{:S(2)}) async-start(), calls=%async_computation.14 | async-start | bytes 7077888 | tf_op jit(solution)/shard_map/all_gather | solution.py:248
  254.0 350.6 %all-gather.19.cloned.1.call-start = ((), (), s32[]{:S(2)}) async-start(), calls=%async_computation.13 | async-start | bytes 7077888 | tf_op jit(solution)/shard_map/all_gather | solution.py:247
  254.7 449.6 %all-gather.23.cloned.1.call-start = ((), (), s32[]{:S(2)}) async-start(), calls=%async_computation.15 | async-start | bytes 7077888 | tf_op jit(solution)/shard_map/all_gather | solution.py:249
  255.5 648.5 %all-reduce.16.cloned.1.call-start = ((), (), s32[]{:S(2)}) async-start(), calls=%async_computation.24 | async-start | bytes 16777216 | tf_op jit(solution)/shard_map/psum | solution.py:130
  404.5 6.0 copy-start.4
  404.5 7.1 copy-start.14
  404.5 8.3 copy-start.15
  404.5 8.3 copy-start.100
  604.6 8.6 copy-start.69
  604.6 8.6 copy-start.124
  604.6 13.7 slice-start.2
  716.8 8.3 copy-start.44
  716.8 8.3 copy-start.123
  725.1 22.4 %slice-start = ((s8[6291456]{0:T(1024)(128)(4,1)}), s8[2097152]{0:T(1024)(128)(4,1)S(1)}, s32[]{:S(2)}) async-start(s8[6291456]{0:T(1024)(128)(4,1)} %bitcast.412), calls=%async_computation.27 | async-start | bytes 4194304
  732.8 6.8 copy-start.125
  732.8 6.8 copy-start.126
  732.9 14.7 slice-start.1
  739.6 8.0 copy-start.130
  739.6 8.0 copy-start.133
  752.7 310.7 %reduce-scatter.13.cloned.1.call-start = ((), (), s32[]{:S(2)}) async-start(), calls=%async_computation.18 | async-start | bytes 1179648 | tf_op jit(solution)/shard_map/reduce_scatter | solution.py:277
  752.8 8.1 copy-start.132
  903.9 7.0 copy-start.12
  903.9 8.3 copy-start.13
  903.9 9.5 copy-start.22
  913.4 6.1 copy-start.67
  913.4 6.1 copy-start.68
  926.6 9.1 copy-start.87
  935.7 9.0 copy-start.65
  953.6 18.5 copy-start.80
  953.6 9.1 copy-start.85
  962.8 9.3 copy-start.110
  962.8 9.3 copy-start.114
  977.3 130.9 %reduce-scatter.11.cloned.1.call-start = ((), (), s32[]{:S(2)}) async-start(), calls=%async_computation.17 | async-start | bytes 1179648 | tf_op jit(solution)/shard_map/reduce_scatter | solution.py:274
  987.6 275.7 %all-reduce.20.cloned.1.call-start = ((), (), s32[]{:S(2)}) async-start(), calls=%async_computation.26 | async-start | bytes 16777216 | tf_op jit(solution)/shard_map/psum | solution.py:112
  990.3 5.8 copy-start.60
  1003.2 332.6 %reduce-scatter.17.cloned.1.call-start = ((), (), s32[]{:S(2)}) async-start(), calls=%async_computation.20 | async-start | bytes 2359296 | tf_op jit(solution)/shard_map/reduce_scatter | solution.py:283
  1010.5 396.2 %reduce-scatter.9.cloned.1.call-start = ((), (), s32[]{:S(2)}) async-start(), calls=%async_computation.16 | async-start | bytes 2359296 | tf_op jit(solution)/shard_map/reduce_scatter | solution.py:271
  1016.9 460.6 %reduce-scatter.15.cloned.1.call-start = ((), (), s32[]{:S(2)}) async-start(), calls=%async_computation.19 | async-start | bytes 2359296 | tf_op jit(solution)/shard_map/reduce_scatter | solution.py:280
  1023.1 5.8 copy-start.70
  1023.1 575.8 %reduce-scatter.21.cloned.1.call-start = ((), (), s32[]{:S(2)}) async-start(), calls=%async_computation.22 | async-start | bytes 7077888 | tf_op jit(solution)/shard_map/reduce_scatter | solution.py:289
  1023.1 5.8 copy-start.131
  1034.6 685.1 %reduce-scatter.19.cloned.1.call-start = ((), (), s32[]{:S(2)}) async-start(), calls=%async_computation.21 | async-start | bytes 7077888 | tf_op jit(solution)/shard_map/reduce_scatter | solution.py:286
  1046.1 795.0 %reduce-scatter.23.cloned.1.call-start = ((), (), s32[]{:S(2)}) async-start(), calls=%async_computation.23 | async-start | bytes 7077888 | tf_op jit(solution)/shard_map/reduce_scatter | solution.py:292
  1291.1 231.5 %copy-start.35 = (bf16[1,512,2048]{2,1,0:T(8,128)(2,1)S(1)}, bf16[1,512,2048]{2,1,0:T(8,128)(2,1)}, u32[]{:S(2)}) copy-start(bf16[1,512,2048]{2,1,0:T(8,128)(2,1)} %get-tuple-element.66) | copy-start | bytes 6291460
  (93 other events, 237.1 us)
Sparse Core Ops, SparseCore 0:
  10.1 42.9 all-gather.10
  55.3 38.9 all-gather.8
  96.4 47.7 all-gather.12
  146.3 47.6 all-gather.14
  195.8 48.8 all-gather.16
  253.4 151.0 all-reduce.17
  406.6 98.8 all-gather.20
  507.7 96.8 all-gather.18
  606.6 97.6 all-gather.22
  752.8 151.0 all-reduce.15
  977.4 64.3 reduce-scatter.12
  1045.0 63.1 reduce-scatter.10
  1111.4 151.8 all-reduce.19
  1266.7 68.9 reduce-scatter.16
  1339.1 67.5 reduce-scatter.8
  1410.1 67.3 reduce-scatter.14
  1480.9 117.9 reduce-scatter.20
  1602.4 117.2 reduce-scatter.18
  1723.3 117.7 reduce-scatter.22
where the time goes:
time: 1860 us; the launch traced here: 1850 us
  waiting for transfers between devices  1410 us (76%)
  matrix products  247 us (13%)
  other arithmetic  98.7 us (5%)
  blocking collectives  43.3 us (2%)
  local copies, waits for them, and re-layouts  30 us (2%)
    psum x1, waiting for transfers between devices, layer_pass(): lax.psum(jnp.dot(hidden, full_dn, preferred_element_type=wide_type).astyp...  154 us
    psum x1, waiting for transfers between devices, layer_pass(): lax.psum(jnp.dot(gated, full_o, preferred_element_type=wide_type), 'tensor')  149 us
    psum x1, waiting for transfers between devices, layer_pass(): grad_second = lax.psum(part_two, 'tensor')  136 us
    reduce_scatter x1, waiting for transfers between devices, shards(): lax.psum_scatter(totals[7].astype(jnp.bfloat16), 'dp', scatter_dimension=...  119 us
    reduce_scatter x1, waiting for transfers between devices, shards(): lax.psum_scatter(totals[5].astype(jnp.bfloat16), 'dp', scatter_dimension=...  118 us
    all_gather x1, waiting for transfers between devices, shards(): lax.all_gather(ffn_gate_weight, 'dp', axis=0, tiled=True)  90.6 us
    all_gather x1, waiting for transfers between devices, shards(): lax.all_gather(ffn_up_weight, 'dp', axis=0, tiled=True)  87.4 us
    all_gather x1, waiting for transfers between devices, shards(): lax.all_gather(ffn_down_weight, 'dp', axis=1, tiled=True)  81 us
  transfers between devices with their start and end apart: 19, of which 18 were waited for; matrix products, arithmetic and copies ran while one was open for 12% of the time, Pallas kernels for 0%

commit v1 on v0

--- a/solution.py
+++ b/solution.py
@@ -3,8 +3,10 @@
 import jax.numpy as jnp
 from jax import lax
 from jax.sharding import PartitionSpec as P
+from jax.lax import all_gather
 
 epsilon = 1e-06
+strings_unite = lambda field_in, axis_key: all_gather(field_in, axis_key).sum(axis=0)
 
 
 def norm_fwd(vector_in):
@@ -109,7 +111,7 @@
     sig_gate = jax.nn.sigmoid(ffn_gate)
     active = ffn_gate * sig_gate
     hidden = (active * ffn_up).astype(low_type)
-    branch_two = lax.psum(
+    branch_two = strings_unite(
         jnp.dot(hidden, full_dn, preferred_element_type=wide_type).astype(jnp.bfloat16), "tensor"
     ).astype(jnp.float32)
     result = (middle + branch_two).astype(low_type)

time: 1860 us -> 1920 us (1.032)
  waiting for transfers between devices: 1410 us -> 1470 us
    psum x1, waiting for transfers between devices: 154 us -> 0.02 us  [layer_pass(): lax.psum(part_one.astype(jnp.bfloat16), 'tensor').astype(jnp.float32)]
    all_gather x0 -> x2, waiting for transfers between devices: none -> 109 us  [all_gather(field_in, axis_key).sum(axis=0)]
    reduce_scatter x1, waiting for transfers between devices: 0.02 us -> 60.5 us  [shards(): lax.psum_scatter(totals[2].astype(jnp.bfloat16), 'dp', scatter_dimension=...]
    reduce_scatter x1, waiting for transfers between devices: 119 us -> 67.1 us  [shards(): lax.psum_scatter(totals[7].astype(jnp.bfloat16), 'dp', scatter_dimension=...]
    reduce_scatter x1, waiting for transfers between devices: 66.7 us -> 92.1 us  [shards(): lax.psum_scatter(totals[6].astype(jnp.bfloat16), 'dp', scatter_dimension=...]
    reduce_scatter x1, waiting for transfers between devices: 41.1 us -> 65.9 us  [shards(): lax.psum_scatter(totals[4].astype(jnp.bfloat16), 'dp', scatter_dimension=...]
    reduce_scatter x1, waiting for transfers between devices: 43.2 us -> 65 us  [shards(): lax.psum_scatter(totals[1].astype(jnp.bfloat16), 'dp', scatter_dimension=...]
  transfers between devices with their start and end apart: 19 -> 21, of which waited for: 18 -> 20; matrix products, arithmetic and copies ran while one was open for 12% -> 12% of each run, Pallas kernels for 0% -> 0%
where the time goes in v1:
time: 1920 us
  waiting for transfers between devices  1470 us (77%)
  matrix products  249 us (13%)
  other arithmetic  114 us (6%)
  blocking collectives  43.2 us (2%)
  local copies, waits for them, and re-layouts  26.1 us (1%)
    psum x1, waiting for transfers between devices, layer_pass(): grad_second = lax.psum(part_two, 'tensor')  151 us
    psum x1, waiting for transfers between devices, layer_pass(): lax.psum(jnp.dot(gated, full_o, preferred_element_type=wide_type), 'tensor')  149 us
    reduce_scatter x1, waiting for transfers between devices, shards(): lax.psum_scatter(totals[5].astype(jnp.bfloat16), 'dp', scatter_dimension=...  119 us
    all_gather x2, waiting for transfers between devices, all_gather(field_in, axis_key).sum(axis=0)  109 us
    reduce_scatter x1, waiting for transfers between devices, shards(): lax.psum_scatter(totals[6].astype(jnp.bfloat16), 'dp', scatter_dimension=...  92.1 us
    all_gather x1, waiting for transfers between devices, shards(): lax.all_gather(ffn_gate_weight, 'dp', axis=0, tiled=True)  90.6 us
    all_gather x1, waiting for transfers between devices, shards(): lax.all_gather(ffn_up_weight, 'dp', axis=0, tiled=True)  87.4 us
    all_gather x1, waiting for transfers between devices, shards(): lax.all_gather(ffn_down_weight, 'dp', axis=1, tiled=True)  80.8 us
  transfers between devices with their start and end apart: 21, of which 20 were waited for; matrix products, arithmetic and copies ran while one was open for 12% of the time, Pallas kernels for 0%

profile of v1, /device:TPU:0, one launch (start us, length us, event | category | flops | bytes accessed | tf_op | source)
XLA Modules:
  0.0 1917.3 jit_solution(16500278229862544576)
XLA Ops:
  19.3 33.9 %all-gather.15.cloned.1.call-done = bf16[2048,256]{1,0:T(8,128)(2,1)} async-done(((bf16[256,256]{1,0:T(8,128)(2,1)}), bf16[2048,256]{1,0:T(8,128)(2,1)}) %all-gather.15.cloned.1.call-update) | async-done | bytes 1048592 | tf_op jit(solution)/shard_map/all_gather | solution.py:245
  59.6 34.7 %all-gather.13.cloned.1.call-done = bf16[2048,256]{1,0:T(8,128)(2,1)} async-done(((bf16[256,256]{1,0:T(8,128)(2,1)}), bf16[2048,256]{1,0:T(8,128)(2,1)}) %all-gather.13.cloned.1.call-update) | async-done | bytes 1048592 | tf_op jit(solution)/shard_map/all_gather | solution.py:246
  98.7 45.6 %all-gather.17.cloned.1.call-done = bf16[2048,512]{1,0:T(8,128)(2,1)} async-done(((bf16[256,512]{1,0:T(8,128)(2,1)}), bf16[2048,512]{1,0:T(8,128)(2,1)}) %all-gather.17.cloned.1.call-update) | async-done | bytes 2097168 | tf_op jit(solution)/shard_map/all_gather | solution.py:244
  144.3 4.4 copy.48
  148.7 3.7 multiply_reduce_fusion.10
  162.5 31.4 %all-gather.19.cloned.1.call-done = bf16[2048,512]{1,0:T(8,128)(2,1)} async-done(((bf16[256,512]{1,0:T(8,128)(2,1)}), bf16[2048,512]{1,0:T(8,128)(2,1)}) %all-gather.19.cloned.1.call-update) | async-done | bytes 2097168 | tf_op jit(solution)/shard_map/all_gather | solution.py:247
  193.9 4.9 fusion.115
  205.0 39.8 %all-gather.21.cloned.1.call-done = bf16[512,2048]{1,0:T(8,128)(2,1)} async-done(((bf16[512,256]{1,0:T(8,128)(2,1)}), bf16[512,2048]{1,0:T(8,128)(2,1)}) %all-gather.21.cloned.1.call-update) | async-done | bytes 2097168 | tf_op jit(solution)/shard_map/all_gather | solution.py:248
  244.7 5.3 fusion.178
  250.0 3.3 fusion.175
  255.6 148.9 %all-reduce.18.cloned.1.call-done = (f32[512,2048]{1,0:T(8,128)}, f32[512,2048]{1,0:T(8,128)}) async-done(((f32[512,2048]{1,0:T(8,128)}, f32[512,2048]{1,0:T(8,128)}), (f32[512,2048]{1,0:T(8,128)}, f32[512,2048]{1,0:T(8,128)})) %all-reduce.18.cloned.1.call-update) | async-done | bytes 8388624 | tf_op jit(solution)/shard_map/psum | solution.py:105
  404.6 5.9 multiply_reduce_fusion.5
  412.9 5.4 multiply_convert_fusion.2
  418.3 87.4 %all-gather.25.cloned.1.call-done = bf16[2048,1536]{1,0:T(8,128)(2,1)} async-done(((bf16[256,1536]{1,0:T(8,128)(2,1)}), bf16[2048,1536]{1,0:T(8,128)(2,1)}) %all-gather.25.cloned.1.call-update) | async-done | bytes 6291472 | tf_op jit(solution)/shard_map/all_gather | solution.py:250
  505.6 8.5 fusion.177
  514.1 90.6 %all-gather.23.cloned.1.call-done = bf16[2048,1536]{1,0:T(8,128)(2,1)} async-done(((bf16[256,1536]{1,0:T(8,128)(2,1)}), bf16[2048,1536]{1,0:T(8,128)(2,1)}) %all-gather.23.cloned.1.call-update) | async-done | bytes 6291472 | tf_op jit(solution)/shard_map/all_gather | solution.py:249
  604.7 8.6 fusion.176
  613.3 5.2 fusion.180
  618.5 5.1 fusion.179
  623.6 80.8 %all-gather.27.cloned.1.call-done = bf16[1536,2048]{1,0:T(8,128)(2,1)} async-done(((bf16[1536,256]{1,0:T(8,128)(2,1)}), bf16[1536,2048]{1,0:T(8,128)(2,1)}) %all-gather.27.cloned.1.call-update) | async-done | bytes 6291472 | tf_op jit(solution)/shard_map/all_gather | solution.py:251
  704.5 11.4 multiply_convert_fusion.4
  717.0 8.5 fusion.186
  725.5 7.7 multiply_convert_fusion.6
  733.2 6.7 fusion.181
  740.0 7.9 convolution_add_fusion.1
  747.9 5.1 convolution_add_fusion
  753.2 151.1 %all-reduce.16.cloned.1.call-done = (f32[512,2048]{1,0:T(8,128)}, f32[512,2048]{1,0:T(8,128)}) async-done(((f32[512,2048]{1,0:T(8,128)}, f32[512,2048]{1,0:T(8,128)}), (f32[512,2048]{1,0:T(8,128)}, f32[512,2048]{1,0:T(8,128)})) %all-reduce.16.cloned.1.call-update) | async-done | bytes 8388624 | tf_op jit(solution)/shard_map/psum | solution.py:132
  904.3 6.9 multiply_reduce_fusion.3
  913.8 6.1 multiply_add_fusion.1
  927.1 9.0 broadcast_multiply_fusion.3
  936.1 8.1 fusion.67
  944.2 5.0 fusion.101
  954.1 9.0 broadcast_multiply_fusion.2
  963.1 8.2 fusion.61
  987.4 3.1 add_convert_fusion.7
  1001.8 3.7 fusion.120
  1008.2 3.2 fusion.52
  1014.5 3.2 fusion.155
  1020.8 8.2 convolution_convert_fusion.1
  1029.1 7.5 convolution_convert_fusion
  1036.7 5.8 fusion.192
  1042.5 5.7 add_convert_fusion.1
  1048.5 5.8 fusion.191
  1054.3 5.6 add_convert_fusion.2
  1060.0 5.7 fusion.37
  1065.8 7.4 add_convert_fusion
  1076.6 4.2 convert_element_type.359
  1083.4 60.5 %reduce-scatter.13.cloned.1.call-done = bf16[256,256]{1,0:T(8,128)(2,1)} async-done(((bf16[2048,256]{1,0:T(8,128)(2,1)}), bf16[256,256]{1,0:T(8,128)(2,1)}) %reduce-scatter.13.cloned.1.call-update) | async-done | bytes 131088 | tf_op jit(solution)/shard_map/reduce_scatter | solution.py:279
  1145.6 65.0 %reduce-scatter.11.cloned.1.call-done = bf16[256,256]{1,0:T(8,128)(2,1)} async-done(((bf16[2048,256]{1,0:T(8,128)(2,1)}), bf16[256,256]{1,0:T(8,128)(2,1)}) %reduce-scatter.11.cloned.1.call-update) | async-done | bytes 131088 | tf_op jit(solution)/shard_map/reduce_scatter | solution.py:276
  1212.2 3.8 multiply_reduce_fusion.2
  1216.0 65.9 %reduce-scatter.17.cloned.1.call-done = bf16[512,256]{1,0:T(8,128)(2,1)} async-done(((bf16[512,2048]{1,0:T(8,128)(2,1)}), bf16[512,256]{1,0:T(8,128)(2,1)}) %reduce-scatter.17.cloned.1.call-update) | async-done | bytes 262160 | tf_op jit(solution)/shard_map/reduce_scatter | solution.py:285
  1283.7 69.3 %reduce-scatter.9.cloned.1.call-done = bf16[256,512]{1,0:T(8,128)(2,1)} async-done(((bf16[2048,512]{1,0:T(8,128)(2,1)}), bf16[256,512]{1,0:T(8,128)(2,1)}) %reduce-scatter.9.cloned.1.call-update) | async-done | bytes 262160 | tf_op jit(solution)/shard_map/reduce_scatter | solution.py:273
  1354.9 68.9 %reduce-scatter.15.cloned.1.call-done = bf16[256,512]{1,0:T(8,128)(2,1)} async-done(((bf16[2048,512]{1,0:T(8,128)(2,1)}), bf16[256,512]{1,0:T(8,128)(2,1)}) %reduce-scatter.15.cloned.1.call-update) | async-done | bytes 262160 | tf_op jit(solution)/shard_map/reduce_scatter | solution.py:282
  1425.6 56.9 %all-gather.29.cloned.1.call-done = bf16[2048,2048]{1,0:T(8,128)(2,1)} async-done(((bf16[512,2048]{1,0:T(8,128)(2,1)}), bf16[2048,2048]{1,0:T(8,128)(2,1)}) %all-gather.29.cloned.1.call-update) | async-done | bytes 8388624 | tf_op jit(solution)/shard_map/all_gather | solution.py:9
  1482.5 7.2 reduce_sum.313
  1489.7 52.5 %all-gather.31.cloned.1.call-done = bf16[2048,2048]{1,0:T(8,128)(2,1)} async-done(((bf16[512,2048]{1,0:T(8,128)(2,1)}), bf16[2048,2048]{1,0:T(8,128)(2,1)}) %all-gather.31.cloned.1.call-update) | async-done | bytes 8388624 | tf_op jit(solution)/shard_map/all_gather | solution.py:9
  1542.2 7.2 reduce_sum.319
  1549.5 18.8 add_bitcast_fusion.1
  1571.7 92.1 %reduce-scatter.21.cloned.1.call-done = bf16[256,1536]{1,0:T(8,128)(2,1)} async-done(((bf16[2048,1536]{1,0:T(8,128)(2,1)}), bf16[256,1536]{1,0:T(8,128)(2,1)}) %reduce-scatter.21.cloned.1.call-update) | async-done | bytes 786448 | tf_op jit(solution)/shard_map/reduce_scatter | solution.py:291
  1666.3 118.9 %reduce-scatter.19.cloned.1.call-done = bf16[256,1536]{1,0:T(8,128)(2,1)} async-done(((bf16[2048,1536]{1,0:T(8,128)(2,1)}), bf16[256,1536]{1,0:T(8,128)(2,1)}) %reduce-scatter.19.cloned.1.call-update) | async-done | bytes 786448 | tf_op jit(solution)/shard_map/reduce_scatter | solution.py:288
  1787.6 43.2 %all-reduce.8 = (f32[2048]{0:T(1024)}, f32[2048]{0:T(1024)}, f32[128]{0:T(128)}, f32[128]{0:T(128)}) all-reduce(f32[2048]{0:T(1024)S(1)} %add.307, f32[2048]{0:T(1024)S(1)} %add.308, f32[128]{0:T(128)S(1)} %add.309, f32[128]{0:T(128)S(1)} %add.310), channel_id=1, replica_groups=mesh['dp'=8,'tensor'=4] {'dp','tensor'}, use_global_device_ids=true, to_apply=%region_44.45 | all-reduce | flops 4352 | bytes 34816 | tf_op jit(solution)/shard_map/psum | solution.py:298
  1830.8 4.3 pad_maximum_fusion.1
  1836.5 4.0 pad_maximum_fusion
  1840.5 67.1 %reduce-scatter.23.cloned.1.call-done = bf16[1536,256]{1,0:T(8,128)(2,1)} async-done(((bf16[1536,2048]{1,0:T(8,128)(2,1)}), bf16[1536,256]{1,0:T(8,128)(2,1)}) %reduce-scatter.23.cloned.1.call-update) | async-done | bytes 786448 | tf_op jit(solution)/shard_map/reduce_scatter | solution.py:294
  (395 shorter events, 121.9 us)
Async XLA Ops:
  7.2 46.0 %all-gather.15.cloned.1.call-start = ((), (), s32[]{:S(2)}) async-start(), calls=%async_computation.9 | async-start | bytes 1179648 | tf_op jit(solution)/shard_map/all_gather | solution.py:245
  7.9 86.4 %all-gather.13.cloned.1.call-start = ((), (), s32[]{:S(2)}) async-start(), calls=%async_computation.8 | async-start | bytes 1179648 | tf_op jit(solution)/shard_map/all_gather | solution.py:246
  8.7 135.6 %all-gather.17.cloned.1.call-start = ((), (), s32[]{:S(2)}) async-start(), calls=%async_computation.10 | async-start | bytes 2359296 | tf_op jit(solution)/shard_map/all_gather | solution.py:244
  9.4 184.5 %all-gather.19.cloned.1.call-start = ((), (), s32[]{:S(2)}) async-start(), calls=%async_computation.11 | async-start | bytes 2359296 | tf_op jit(solution)/shard_map/all_gather | solution.py:247
  10.0 234.7 %all-gather.21.cloned.1.call-start = ((), (), s32[]{:S(2)}) async-start(), calls=%async_computation.12 | async-start | bytes 2359296 | tf_op jit(solution)/shard_map/all_gather | solution.py:248
  10.6 394.0 %all-reduce.18.cloned.1.call-start = ((), (), s32[]{:S(2)}) async-start(), calls=%async_computation.27 | async-start | bytes 16777216 | tf_op jit(solution)/shard_map/psum | solution.py:105
  13.6 41.0 %copy-start.94 = (f32[2048]{0:T(1024)S(1)}, f32[2048]{0:T(1024)}, u32[]{:S(2)}) copy-start(f32[2048]{0:T(1024)} %param.25) | copy-start | bytes 24580
  18.2 138.5 %copy-start.34 = (f32[512,128]{0,1:T(8,128)}, f32[512,128]{0,1:T(8,128)S(1)}, u32[]{:S(2)}) copy-start(f32[512,128]{0,1:T(8,128)S(1)} %get-tuple-element.86) | copy-start | bytes 786436
  18.2 138.5 %copy-start.44 = (f32[512,128]{0,1:T(8,128)}, f32[512,128]{0,1:T(8,128)S(1)}, u32[]{:S(2)}) copy-start(f32[512,128]{0,1:T(8,128)S(1)} %get-tuple-element.87) | copy-start | bytes 786436
  19.2 136.2 %copy-start.36 = (f32[512,128]{0,1:T(8,128)}, f32[512,128]{0,1:T(8,128)S(1)}, u32[]{:S(2)}) copy-start(f32[512,128]{0,1:T(8,128)S(1)} %get-tuple-element.88) | copy-start | bytes 786436
  19.2 136.2 %copy-start.46 = (f32[512,128]{0,1:T(8,128)}, f32[512,128]{0,1:T(8,128)S(1)}, u32[]{:S(2)}) copy-start(f32[512,128]{0,1:T(8,128)S(1)} %get-tuple-element.89) | copy-start | bytes 786436
  19.3 174.6 %copy-start.98 = (f32[512]{0:T(512)}, f32[512]{0:T(512)S(1)}, u32[]{:S(2)}) copy-start(f32[512]{0:T(512)S(1)} %get-tuple-element.129) | copy-start | bytes 6148
  19.3 180.5 %copy-start.96 = (f32[512]{0:T(512)}, f32[512]{0:T(512)S(1)}, u32[]{:S(2)}) copy-start(f32[512]{0:T(512)S(1)} %get-tuple-element.128) | copy-start | bytes 6148
  59.4 98.4 %copy-start.73 = (bf16[512,2,128,1]{0,2,3,1:T(8,128)(2,1)}, bf16[512,2,128,1]{0,2,3,1:T(8,128)(2,1)S(1)}, u32[]{:S(2)}) copy-start(bf16[512,2,128,1]{0,2,3,1:T(8,128)(2,1)S(1)} %fusion.131) | copy-start | bytes 786436
  59.6 96.2 %copy-start.75 = (bf16[512,2,128,1]{0,2,3,1:T(8,128)(2,1)}, bf16[512,2,128,1]{0,2,3,1:T(8,128)(2,1)S(1)}, u32[]{:S(2)}) copy-start(bf16[512,2,128,1]{0,2,3,1:T(8,128)(2,1)S(1)} %fusion.132) | copy-start | bytes 786436
  97.7 101.1 %copy-start.79 = (bf16[512,256]{0,1:T(8,128)(2,1)}, bf16[512,256]{0,1:T(8,128)(2,1)S(1)}, u32[]{:S(2)}) copy-start(bf16[512,256]{0,1:T(8,128)(2,1)S(1)} %convolution_convert_fusion.4) | copy-start | bytes 786436
  162.5 36.3 %copy-start.55 = (f32[2,128,2,512]{3,1,2,0:T(8,128)}, f32[2,128,2,512]{3,1,2,0:T(8,128)S(1)}, u32[]{:S(2)}) copy-start(f32[2,128,2,512]{3,1,2,0:T(8,128)S(1)} %fusion.68) | copy-start | bytes 3145732
  198.8 51.2 %copy-start.52 = (bf16[512,512]{0,1:T(8,128)(2,1)}, bf16[512,512]{0,1:T(8,128)(2,1)S(1)}, u32[]{:S(2)}) copy-start(bf16[512,512]{0,1:T(8,128)(2,1)S(1)} %get-tuple-element.118) | copy-start | bytes 1572868
  204.9 48.4 %copy-start.65 = (bf16[512,512]{0,1:T(8,128)(2,1)}, bf16[512,512]{0,1:T(8,128)(2,1)S(1)}, u32[]{:S(2)}) copy-start(bf16[512,512]{0,1:T(8,128)(2,1)S(1)} %get-tuple-element.122) | copy-start | bytes 1572868
  244.7 5.3 copy-start.20
  253.4 252.3 %all-gather.25.cloned.1.call-start = ((), (), s32[]{:S(2)}) async-start(), calls=%async_computation.14 | async-start | bytes 7077888 | tf_op jit(solution)/shard_map/all_gather | solution.py:250
  254.1 350.6 %all-gather.23.cloned.1.call-start = ((), (), s32[]{:S(2)}) async-start(), calls=%async_computation.13 | async-start | bytes 7077888 | tf_op jit(solution)/shard_map/all_gather | solution.py:249
  254.9 449.6 %all-gather.27.cloned.1.call-start = ((), (), s32[]{:S(2)}) async-start(), calls=%async_computation.15 | async-start | bytes 7077888 | tf_op jit(solution)/shard_map/all_gather | solution.py:251
  255.6 648.7 %all-reduce.16.cloned.1.call-start = ((), (), s32[]{:S(2)}) async-start(), calls=%async_computation.26 | async-start | bytes 16777216 | tf_op jit(solution)/shard_map/psum | solution.py:132
  404.6 6.0 copy-start.4
  404.6 7.1 copy-start.13
  404.6 8.3 copy-start.14
  404.6 8.3 copy-start.85
  604.7 8.6 copy-start.58
  604.7 8.6 copy-start.109
  604.7 13.8 slice-start.2
  613.3 5.2 slice-start.3
  717.0 8.5 copy-start.42
  717.0 8.5 copy-start.108
  725.5 22.4 %slice-start = ((s8[6291456]{0:T(1024)(128)(4,1)}), s8[2097152]{0:T(1024)(128)(4,1)S(1)}, s32[]{:S(2)}) async-start(s8[6291456]{0:T(1024)(128)(4,1)} %bitcast.416), calls=%async_computation.29 | async-start | bytes 4194304
  733.2 6.8 copy-start.110
  733.2 6.8 copy-start.111
  733.2 14.7 slice-start.1
  739.9 7.9 copy-start.114
  739.9 7.9 copy-start.117
  753.1 323.5 %all-reduce.20.cloned.1.call-start = ((), (), s32[]{:S(2)}) async-start(), calls=%async_computation.28 | async-start | bytes 8388608 | tf_op jit(solution)/shard_map/psum | solution.py:191
  904.3 7.0 copy-start.11
  904.3 8.3 copy-start.12
  904.3 9.5 copy-start.21
  913.8 6.1 copy-start.56
  913.8 6.1 copy-start.57
  954.1 9.0 copy-start.74
  990.6 153.4 %reduce-scatter.13.cloned.1.call-start = ((), (), s32[]{:S(2)}) async-start(), calls=%async_computation.18 | async-start | bytes 1179648 | tf_op jit(solution)/shard_map/reduce_scatter | solution.py:279
  996.3 214.2 %reduce-scatter.11.cloned.1.call-start = ((), (), s32[]{:S(2)}) async-start(), calls=%async_computation.17 | async-start | bytes 1179648 | tf_op jit(solution)/shard_map/reduce_scatter | solution.py:276
  1001.7 280.3 %reduce-scatter.17.cloned.1.call-start = ((), (), s32[]{:S(2)}) async-start(), calls=%async_computation.20 | async-start | bytes 2359296 | tf_op jit(solution)/shard_map/reduce_scatter | solution.py:285
  1008.1 345.0 %reduce-scatter.9.cloned.1.call-start = ((), (), s32[]{:S(2)}) async-start(), calls=%async_computation.16 | async-start | bytes 2359296 | tf_op jit(solution)/shard_map/reduce_scatter | solution.py:273
  1014.2 409.6 %reduce-scatter.15.cloned.1.call-start = ((), (), s32[]{:S(2)}) async-start(), calls=%async_computation.19 | async-start | bytes 2359296 | tf_op jit(solution)/shard_map/reduce_scatter | solution.py:282
  1020.8 461.8 %all-gather.29.cloned.1.call-start = ((), (), s32[]{:S(2)}) async-start(), calls=%async_computation.24 | async-start | bytes 10485760 | tf_op jit(solution)/shard_map/all_gather | solution.py:9
  1020.8 8.3 copy-start.116
  1029.0 513.2 %all-gather.31.cloned.1.call-start = ((), (), s32[]{:S(2)}) async-start(), calls=%async_computation.25 | async-start | bytes 10485760 | tf_op jit(solution)/shard_map/all_gather | solution.py:9
  1036.6 5.9 copy-start.59
  1036.6 627.3 %reduce-scatter.21.cloned.1.call-start = ((), (), s32[]{:S(2)}) async-start(), calls=%async_computation.22 | async-start | bytes 7077888 | tf_op jit(solution)/shard_map/reduce_scatter | solution.py:291
  1036.6 5.8 copy-start.115
  1048.2 736.9 %reduce-scatter.19.cloned.1.call-start = ((), (), s32[]{:S(2)}) async-start(), calls=%async_computation.21 | async-start | bytes 7077888 | tf_op jit(solution)/shard_map/reduce_scatter | solution.py:288
  1048.5 5.8 copy-start.113
  1060.0 847.6 %reduce-scatter.23.cloned.1.call-start = ((), (), s32[]{:S(2)}) async-start(), calls=%async_computation.23 | async-start | bytes 7077888 | tf_op jit(solution)/shard_map/reduce_scatter | solution.py:294
  1060.0 5.8 copy-start.43
  1568.2 262.6 %copy-start.33 = (bf16[1,512,2048]{2,1,0:T(8,128)(2,1)S(1)}, bf16[1,512,2048]{2,1,0:T(8,128)(2,1)}, u32[]{:S(2)}) copy-start(bf16[1,512,2048]{2,1,0:T(8,128)(2,1)} %get-tuple-element.64) | copy-start | bytes 6291460
  1830.8 5.7 copy-start.25
  (79 other events, 176.9 us)
Sparse Core Ops, SparseCore 0:
  10.1 42.9 all-gather.14
  55.3 38.9 all-gather.12
  96.4 47.7 all-gather.16
  146.3 47.6 all-gather.18
  195.8 48.8 all-gather.20
  253.5 151.0 all-reduce.17
  406.8 98.8 all-gather.24
  507.8 96.8 all-gather.22
  606.8 97.6 all-gather.26
  753.2 151.0 all-reduce.15
  990.7 85.6 all-reduce.19
  1079.6 64.3 reduce-scatter.12
  1147.4 63.1 reduce-scatter.10
  1213.9 67.9 reduce-scatter.16
  1285.3 67.6 reduce-scatter.8
  1356.5 67.2 reduce-scatter.14
  1425.2 57.2 all-gather.28
  1483.9 58.2 all-gather.30
  1545.8 117.9 reduce-scatter.20
  1667.9 117.2 reduce-scatter.18
  1788.8 118.7 reduce-scatter.22
